TPU v7x, 32 devices: a whole 2x2x4 slice. The times are simulated.
32 devices in a mesh: dp: 16 (over z, y, core), ctx: 2 (over x).
Axes of the slice: x: 2, y: 2, z: 4, core: 2. Of those that a mesh axis runs over, the one named last changes fastest.
Arguments:
- conv_input: bfloat16 [16, 256, 4096], P('dp', 'ctx'), may hold values from -6 to 6
- gate_value: bfloat16 [16, 256, 4096], P('dp', 'ctx'), may hold values from -6 to 6
- out_grad: bfloat16 [16, 256, 4096], P('dp', 'ctx'), may hold values from -6 to 6
- filter_taps: bfloat16 [128, 4096], P('dp'), may hold values from -0.5 to 0.5
Outputs:
- input_grad: bfloat16 [16, 256, 4096], P('dp', 'ctx')
- filter_grad: float32 [128, 4096], P('dp')
All inputs are finite; a program needn't handle non-finite values.
Results may differ from a plain program's by a relative error of at most 0.0051.
Values may be sent and summed in bfloat16 or wider, within the bound.
A program may use at most 64 MiB of HBM per device.

v0:
```python
import math

import jax
import jax.numpy as jnp
from jax import lax
from jax.sharding import PartitionSpec as P

TAPS = 128


def from_behind(block, axis, distance):
    devices = range(lax.axis_size(axis))
    route = [(i - distance, i) for i in devices if i - distance in devices]
    return lax.ppermute(block, axis, route)


def correlate(signal, kernel):
    return lax.conv_general_dilated(
        signal[None],
        kernel[:, None, :],
        (1,),
        "VALID",
        dimension_numbers=("NWC", "WIO", "NWC"),
        feature_group_count=signal.shape[1],
        preferred_element_type=jnp.float32,
    )[0]


def shards(conv_input, gate_value, out_grad, filter_taps):
    inputs = conv_input[0]
    rows = inputs.shape[0]
    mixed = (out_grad[0].astype(jnp.float32) * gate_value[0].astype(jnp.float32)).astype(
        jnp.bfloat16
    )
    rim_rows = from_behind(mixed[: TAPS - 1], "ctx", -1)
    grad_ext = jnp.concatenate([mixed, rim_rows], 0)
    partial_grad = correlate(grad_ext, inputs)
    full_taps = lax.all_gather(filter_taps, "dp", axis=0, tiled=True)
    back_sum = correlate(grad_ext, full_taps)
    summed = lax.psum(partial_grad, "ctx")
    shard_grad = lax.psum_scatter(summed, "dp", scatter_dimension=0, tiled=True)
    tokens_all = rows * lax.axis_size("ctx") * lax.axis_size("dp")
    scale_factor = 1.0 / math.sqrt(tokens_all)
    return (back_sum.astype(jnp.bfloat16)[None], shard_grad * scale_factor)


def solution(mesh):
    in_specs = (P("dp", "ctx", None), P("dp", "ctx", None), P("dp", "ctx", None), P("dp", None))
    out_specs = (P("dp", "ctx", None), P("dp", None))
    return jax.shard_map(shards, mesh=mesh, in_specs=in_specs, out_specs=out_specs, check_vma=False)
```

profile of v0, /device:TPU:0, one launch (start us, length us, event | category | flops | bytes accessed | tf_op | source)
XLA Modules:
  0.0 211.5 jit_solution(7849527368872966788)
XLA Ops:
  7.2 0.0 copy-start
  7.2 0.0 reduce-scatter.2.cloned.1.call-start
  7.2 1.9 multiply_convert_fusion
  9.2 0.1 slice_bitcast_fusion
  9.2 1.3 collective-permute-start
  10.5 26.2 %collective-permute-done = bf16[127,4096]{1,0:T(8,128)(2,1)S(1)} collective-permute-done((bf16[127,4096]{1,0:T(8,128)(2,1)S(1)}, bf16[127,4096]{1,0:T(8,128)(2,1)S(1)}, u32[]{:S(2)}, u32[]{:S(2)}) %collective-permute-start) | collective-permute-done | bytes 1040416 | tf_op jit(solution)/shard_map/ppermute | solution.py:14
  36.7 0.2 maximum_bitcast_fusion
  36.9 0.0 copy-done
  36.9 30.1 %fusion = f32[1,128,4096]{2,0,1:T(1,128)S(1)} fusion(bf16[1,255,4096]{2,1,0:T(8,128)(2,1)S(1)} %maximum_bitcast_fusion, bf16[128,1,4096]{2,0,1:T(8,128)(2,1)S(1)} %bitcast.10), kind=kOutput, calls=%fused_computation.1 | convolution fusion | flops 134217728 | bytes 5234688 | tf_op jit(solution)/shard_map/conv_general_dilated | solution.py:18
  67.0 3.0 %copy.23 = f32[1,128,4096]{2,1,0:T(8,128)} copy(f32[1,128,4096]{2,0,1:T(1,128)S(1)} %fusion) | data formatting | bytes 4194304
  70.0 0.0 reduce-scatter.2.cloned.1.call-update
  70.0 0.0 all-gather.2.cloned.1.call-start
  70.1 0.7 all-gather.2.cloned.1.call-update
  70.8 0.0 all-reduce.2.cloned.1.call-start
  70.8 62.3 %reduce-scatter.2.cloned.1.call-done = f32[8,4096]{1,0:T(8,128)} async-done(((f32[128,4096]{1,0:T(8,128)}), f32[8,4096]{1,0:T(8,128)}) %reduce-scatter.2.cloned.1.call-update) | async-done | bytes 131088 | tf_op jit(solution)/shard_map/reduce_scatter | solution.py:41
  133.1 0.0 all-reduce.2.cloned.1.call-update
  133.2 39.0 %all-gather.2.cloned.1.call-done = bf16[128,4096]{1,0:T(8,128)(2,1)} async-done(((bf16[8,4096]{1,0:T(8,128)(2,1)}), bf16[128,4096]{1,0:T(8,128)(2,1)}) %all-gather.2.cloned.1.call-update) | async-done | bytes 1048592 | tf_op jit(solution)/shard_map/all_gather | solution.py:38
  172.2 29.1 %convolution_convert_fusion = bf16[1,128,4096]{2,0,1:T(2,128)(2,1)S(1)} fusion(bf16[1,255,4096]{2,1,0:T(8,128)(2,1)S(1)} %maximum_bitcast_fusion, bf16[128,1,4096]{2,0,1:T(8,128)(2,1)} %bitcast.13), kind=kOutput, calls=%fused_computation | convolution fusion | flops 134742016 | bytes 4186112 | tf_op jit(solution)/shard_map/conv_general_dilated | solution.py:18
  201.3 2.1 copy.12
  203.4 0.0 all-reduce.2.cloned.1.call-done
  203.4 1.6 broadcast_multiply_fusion
Async XLA Ops:
  7.2 29.8 %copy-start = (bf16[1,128,4096]{2,1,0:T(8,128)(2,1)S(1)}, bf16[1,128,4096]{2,1,0:T(8,128)(2,1)}, u32[]{:S(2)}) copy-start(bf16[1,128,4096]{2,1,0:T(8,128)(2,1)} %param.4) | copy-start | bytes 3145732
  7.2 126.0 %reduce-scatter.2.cloned.1.call-start = ((), (), s32[]{:S(2)}) async-start(), calls=%async_computation.2 | async-start | bytes 2228224 | tf_op jit(solution)/shard_map/reduce_scatter | solution.py:41
  9.2 27.5 %collective-permute-start = (bf16[127,4096]{1,0:T(8,128)(2,1)S(1)}, bf16[127,4096]{1,0:T(8,128)(2,1)S(1)}, u32[]{:S(2)}, u32[]{:S(2)}) collective-permute-start(bf16[127,4096]{1,0:T(8,128)(2,1)S(1)} %slice_bitcast_fusion), channel_id=1, source_target_pairs={{1,0},{3,2},{5,4},{7,6},{9,8},{11,10},{13,12},{15,14},{17,16},{19,... | collective-permute-start | bytes 3121160 | tf_op jit(solution)/shard_map/ppermute | solution.py:14
  70.0 102.1 %all-gather.2.cloned.1.call-start = ((), (), s32[]{:S(2)}) async-start(), calls=%async_computation.1 | async-start | bytes 1114112 | tf_op jit(solution)/shard_map/all_gather | solution.py:38
  70.8 132.6 %all-reduce.2.cloned.1.call-start = ((), (), s32[]{:S(2)}) async-start(), calls=%async_computation.3 | async-start | bytes 262144 | tf_op jit(solution)/shard_map/psum | solution.py:40
Sparse Core Ops, SparseCore 0:
  70.2 62.9 reduce-scatter.1
  135.3 36.8 all-gather.1
  174.4 20.4 all-reduce.1
where the time goes:
time: 212 us; the launch traced here: 211 us
  waiting for transfers between devices  128 us (60%)
  matrix products  59.2 us (28%)
  between operations  13.8 us (7%)
  local copies, waits for them, and re-layouts  5.18 us (2%)
  other arithmetic  3.71 us (2%)
    reduce_scatter x1, waiting for transfers between devices, shards(): shard_grad = lax.psum_scatter(summed, 'dp', scatter_dimension=0, tiled=True)  62.3 us
    conv_general_dilated x2, matrix products, correlate(): lax.conv_general_dilated(signal[None], kernel[:, None, :], (1,), 'VALID',...  59.2 us
    all_gather x1, waiting for transfers between devices, shards(): full_taps = lax.all_gather(filter_taps, 'dp', axis=0, tiled=True)  39 us
    ppermute x1, waiting for transfers between devices, from_behind(): return lax.ppermute(block, axis, route)  26.2 us
    unnamed x4, local copies, waits for them, and re-layouts  5.1 us
  transfers between devices with their start and end apart: 4, of which 3 were waited for; matrix products, arithmetic and copies ran while one was open for 15% of the time, Pallas kernels for 0%

commit v1 on v0

v1 whole, which is shorter than its diff:
```python
import math

import jax
import jax.numpy as jnp
import numpy as np
from jax import lax
from jax.sharding import PartitionSpec as P


def split(values):
    high = values.astype(jnp.bfloat16)
    return high, (values - high.astype(np.float32)).astype(jnp.bfloat16)


def transforms(length):
    half = length // 2
    angle = np.pi * np.outer(2 * np.arange(half) + 1, np.arange(length)) / length
    forward = np.concatenate([np.cos(angle), -np.sin(angle)], 0)
    inverse = np.concatenate([np.cos(angle), -np.sin(angle)], 0).T / half
    return split(forward.astype(np.float32)), split(inverse.astype(np.float32))


def dot(a, b):
    return lax.dot_general(a, b, (((1,), (0,)), ((), ())), preferred_element_type=jnp.float32)


def shards(conv_input, gate_value, out_grad, filter_taps):
    inputs = conv_input[0]
    rows = inputs.shape[0]
    taps = filter_taps.shape[0] * lax.axis_size("dp")
    (fh, fl), (bh, bl) = transforms(rows + taps)
    half = (rows + taps) // 2
    mixed = (out_grad[0].astype(jnp.float32) * gate_value[0].astype(jnp.float32)).astype(
        jnp.bfloat16
    )
    devices = lax.axis_size("ctx")
    rim = lax.ppermute(mixed[:taps], "ctx", [(i + 1, i) for i in range(devices - 1)])
    full_taps = lax.all_gather(filter_taps, "dp", axis=0, tiled=True)

    def spectrum(x, first=0):
        n = x.shape[0]
        s = dot(fh[:, first : first + n], x) + dot(fl[:, first : first + n], x)
        return s[:half], s[half:]

    def back(re, im, n):
        s = jnp.concatenate([re, im], 0)
        high = s.astype(jnp.bfloat16)
        low = (s - high.astype(jnp.float32)).astype(jnp.bfloat16)
        return dot(bh[:n], high) + dot(bl[:n], high) + dot(bh[:n], low)

    xr, xi = spectrum(inputs)
    gr0, gi0 = spectrum(mixed)
    gr1, gi1 = spectrum(rim, rows)
    gr, gi = gr0 + gr1, gi0 + gi1
    partial = back(xr * gr + xi * gi, xr * gi - xi * gr, taps)
    hr, hi = spectrum(full_taps)
    grad = back(hr * gr + hi * gi, hr * gi - hi * gr, rows)
    shard_grad = lax.psum(lax.psum_scatter(partial, "dp", scatter_dimension=0, tiled=True), "ctx")
    tokens_all = rows * devices * lax.axis_size("dp")
    return (grad.astype(jnp.bfloat16)[None], shard_grad * (1.0 / math.sqrt(tokens_all)))


def solution(mesh):
    in_specs = (P("dp", "ctx", None), P("dp", "ctx", None), P("dp", "ctx", None), P("dp", None))
    out_specs = (P("dp", "ctx", None), P("dp", None))
    return jax.shard_map(shards, mesh=mesh, in_specs=in_specs, out_specs=out_specs, check_vma=False)
```

time: 212 us -> 204 us (0.962)
  matrix products: 59.2 us -> 18.2 us
  waiting for transfers between devices: 128 us -> 148 us
  other arithmetic: 3.71 us -> 11.1 us
  local copies, waits for them, and re-layouts: 5.18 us -> 10.7 us
    reduce_scatter x1 -> x0, waiting for transfers between devices: 62.3 us -> none  [shards(): shard_grad = lax.psum_scatter(summed, 'dp', scatter_dimension=0, tiled=True)]
    conv_general_dilated x2 -> x0, matrix products: 59.2 us -> none  [correlate(): lax.conv_general_dilated(signal[None], kernel[:, None, :], (1,), 'VALID',...]
    psum x1, waiting for transfers between devices: 0.01 us -> 57.7 us  [shards(): lax.psum(lax.psum_scatter(partial, 'dp', scatter_dimension=0, tiled=True)...]
    unnamed x3 -> x4, waiting for transfers between devices: 0.73 us -> 56.1 us
    all_gather x1, waiting for transfers between devices: 39 us -> 11.2 us  [shards(): full_taps = lax.all_gather(filter_taps, 'dp', axis=0, tiled=True)]
    dot_general x0 -> x14, matrix products: none -> 18.2 us  [dot(): lax.dot_general(a, b, (((1,), (0,)), ((), ())), preferred_element_type=jn...]
    add x0 -> x2, other arithmetic: none -> 7.41 us  [the longest x1 4.21 us: shards(): grad = back(hr * gr + hi * gi, hr * gi - hi * gr, rows)]
    unnamed x4 -> x32, local copies, waits for them, and re-layouts: 5.1 us -> 10.7 us
  transfers between devices with their start and end apart: 4 -> 4, of which waited for: 3 -> 4; matrix products, arithmetic and copies ran while one was open for 15% -> 8% of each run, Pallas kernels for 0% -> 0%
where the time goes in v1:
time: 204 us
  waiting for transfers between devices  148 us (73%)
  matrix products  18.2 us (9%)
  between operations  14 us (7%)
  other arithmetic  11.1 us (5%)
  local copies, waits for them, and re-layouts  10.7 us (5%)
    psum x1, waiting for transfers between devices, shards(): lax.psum(lax.psum_scatter(partial, 'dp', scatter_dimension=0, tiled=True)...  57.7 us
    unnamed x4, waiting for transfers between devices  56.1 us
    ppermute x1, waiting for transfers between devices, shards(): lax.ppermute(mixed[:taps], 'ctx', [(i + 1, i) for i in range(devices - 1)])  23 us
    dot_general x14, matrix products, dot(): lax.dot_general(a, b, (((1,), (0,)), ((), ())), preferred_element_type=jn...  18.2 us
    all_gather x1, waiting for transfers between devices, shards(): full_taps = lax.all_gather(filter_taps, 'dp', axis=0, tiled=True)  11.2 us
    unnamed x32, local copies, waits for them, and re-layouts  10.7 us
    add x1, other arithmetic, shards(): grad = back(hr * gr + hi * gi, hr * gi - hi * gr, rows)  4.21 us
  transfers between devices with their start and end apart: 4, of which 4 were waited for; matrix products, arithmetic and copies ran while one was open for 8% of the time, Pallas kernels for 0%

profile of v1, /device:TPU:0, one launch (start us, length us, event | category | flops | bytes accessed | tf_op | source)
XLA Modules:
  0.0 203.6 jit_solution(12447030233872739120)
XLA Ops:
  7.2 1.9 fusion.7
  9.1 1.3 collective-permute-start
  10.5 0.7 fusion.26
  11.2 0.7 fusion.9
  11.9 0.1 copy-done.9
  12.0 0.7 fusion.1
  12.8 0.7 convolution_add_fusion.2
  13.6 23.0 %collective-permute-done = bf16[128,4096]{1,0:T(8,128)(2,1)S(1)} collective-permute-done((bf16[128,4096]{1,0:T(8,128)(2,1)S(1)}, bf16[128,4096]{1,0:T(8,128)(2,1)S(1)}, u32[]{:S(2)}, u32[]{:S(2)}) %collective-permute-start) | collective-permute-done | bytes 1048608 | tf_op jit(solution)/shard_map/ppermute | solution.py:37
  36.6 0.7 fusion.27
  37.3 0.7 fusion
  38.0 3.2 %multiply_add_fusion = (f32[128,4096]{1,0:T(8,128)}, f32[128,4096]{1,0:T(8,128)}, f32[128,4096]{1,0:T(8,128)}) fusion(f32[256,4096]{1,0:T(8,128)S(1)} %convolution_add_fusion.2, f32[256,4096]{1,0:T(8,128)S(1)} %fusion, f32[256,4096]{1,0:T(8,128)S(1)} %fusion.1), kind=kLoop, calls=%fused_computation.22 | loop fusion | flops 2621440 | bytes 18874368 | tf_op jit(solution)/shard_map/add | solution.py:55
  41.2 11.2 %all-gather.2.cloned.1.call-done = bf16[128,4096]{1,0:T(8,128)(2,1)} async-done(((bf16[8,4096]{1,0:T(8,128)(2,1)}), bf16[128,4096]{1,0:T(8,128)(2,1)}) %all-gather.2.cloned.1.call-update) | async-done | bytes 1048592 | tf_op jit(solution)/shard_map/all_gather | solution.py:38
  52.4 2.0 fusion.25
  54.4 0.7 convolution_add_fusion.3
  55.2 1.4 copy-done.3
  56.6 0.7 copy-done.6
  57.3 4.2 %multiply_add_fusion.1 = (f32[128,4096]{1,0:T(8,128)S(1)}, f32[128,4096]{1,0:T(8,128)}, f32[128,4096]{1,0:T(8,128)S(1)}) fusion(f32[128,4096]{1,0:T(8,128)S(1)} %copy-done.6, f32[128,4096]{1,0:T(8,128)} %get-tuple-element.8, f32[256,4096]{1,0:T(8,128)S(1)} %convolution_add_fusion.3, f32[256,4096]{1,0:T(8,128)S(1)} %copy-done.3), kind=kLoop, calls=%fused_computation.24 | loop fusion | flops 4718592 | bytes 18874368 | tf_op jit(solution)/shard_map/add | solution.py:57
  61.5 0.8 fusion.17
  62.3 0.1 copy-done.11
  62.3 0.8 convolution_add_fusion.5
  63.1 2.1 %fusion.2 = f32[128,4096]{0,1:T(8,128)} fusion(f32[4096,128]{1,0:T(8,128)S(1)} %convolution_add_fusion.5, bf16[128,256]{1,0:T(8,128)(2,1)S(1)} %copy-done.8, f32[128,4096]{1,0:T(8,128)S(1)} %get-tuple-element.11, f32[128,4096]{1,0:T(8,128)S(1)} %copy-done.5), kind=kOutput, calls=%fused_computation.7 | convolution fusion | flops 274202624 | bytes 8454144 | tf_op jit(solution)/shard_map/dot_general | solution.py:24
  65.2 3.0 %copy.24 = f32[128,4096]{1,0:T(8,128)} copy(f32[128,4096]{0,1:T(8,128)} %fusion.2) | data formatting | bytes 4194304
  68.2 0.2 all-reduce.2.cloned.1.call-start
  68.4 2.5 %fusion.13 = f32[4096,128]{1,0:T(8,128)S(1)} fusion(bf16[128,256]{1,0:T(8,128)(2,1)S(1)} %copy-done.8, f32[128,4096]{1,0:T(8,128)} %get-tuple-element.10, f32[128,4096]{1,0:T(8,128)S(1)} %get-tuple-element.9), kind=kOutput, calls=%fused_computation.31 | convolution fusion | flops 272629760 | bytes 6356992 | tf_op jit(solution)/shard_map/dot_general | solution.py:24
  70.9 2.1 %convolution_add_fusion.7 = f32[4096,128]{1,0:T(8,128)} fusion(f32[4096,128]{1,0:T(8,128)S(1)} %fusion.13, bf16[128,256]{1,0:T(8,128)(2,1)S(1)} %copy-done.11, f32[128,4096]{1,0:T(8,128)S(1)} %copy-done.4, f32[128,4096]{1,0:T(8,128)S(1)} %get-tuple-element.9), kind=kOutput, calls=%fused_computation.10 | convolution fusion | flops 273154048 | bytes 8454144 | tf_op jit(solution)/shard_map/dot_general | solution.py:24
  73.0 56.1 %reduce-scatter.4.cloned.1.call-done = f32[8,4096]{1,0:T(8,128)} async-done(((f32[128,4096]{1,0:T(8,128)}), f32[8,4096]{1,0:T(8,128)}) %reduce-scatter.4.cloned.1.call-update) | async-done | bytes 131088
  129.1 2.9 %copy.25 = f32[8,4096]{0,1:T(8,128)} copy(f32[8,4096]{1,0:T(8,128)} %reduce-scatter.4.cloned.1.call-done) | data formatting | bytes 262144
  132.0 3.0 %fusion.4 = bf16[1,128,4096]{1,2,0:T(8,128)(2,1)S(1)} fusion(f32[4096,128]{1,0:T(8,128)} %convolution_add_fusion.7, bf16[128,256]{1,0:T(8,128)(2,1)S(1)} %copy-done.8, f32[128,4096]{1,0:T(8,128)} %get-tuple-element.10, f32[128,4096]{1,0:T(8,128)S(1)} %get-tuple-element.9), kind=kOutput, calls=%fused_computation.12 | convolution fusion | flops 274726912 | bytes 7405568 | tf_op jit(solution)/shard_map/dot_general | solution.py:24
  135.0 1.3 copy.22
  136.3 57.7 %all-reduce.2.cloned.1.call-done = f32[8,4096]{0,1:T(8,128)} async-done(((f32[8,4096]{0,1:T(8,128)}), f32[8,4096]{0,1:T(8,128)}) %all-reduce.2.cloned.1.call-update) | async-done | bytes 131088 | tf_op jit(solution)/shard_map/psum | solution.py:58
  194.0 1.8 broadcast_multiply_fusion
  195.8 1.2 copy.23
  (29 shorter events, 0.2 us)
Async XLA Ops:
  7.2 4.0 %copy-start = (bf16[1,128,4096]{2,1,0:T(8,128)(2,1)S(1)}, bf16[1,128,4096]{2,1,0:T(8,128)(2,1)}, u32[]{:S(2)}) copy-start(bf16[1,128,4096]{2,1,0:T(8,128)(2,1)} %param.18) | copy-start | bytes 3145732
  7.2 3.3 %copy-start.10 = (bf16[256,128]{1,0:T(8,128)(2,1)S(1)}, bf16[256,128]{1,0:T(8,128)(2,1)}, u32[]{:S(2)}) copy-start(bf16[256,128]{1,0:T(8,128)(2,1)} %constant.14.clone) | copy-start | bytes 196612
  7.2 45.2 %all-gather.2.cloned.1.call-start = ((), (), s32[]{:S(2)}) async-start(), calls=%async_computation.1 | async-start | bytes 1114112 | tf_op jit(solution)/shard_map/all_gather | solution.py:38
  9.1 27.5 %collective-permute-start = (bf16[128,4096]{1,0:T(8,128)(2,1)S(1)}, bf16[128,4096]{1,0:T(8,128)(2,1)S(1)}, u32[]{:S(2)}, u32[]{:S(2)}) collective-permute-start(bf16[128,4096]{1,0:T(8,128)(2,1)S(1)} %fusion.7), channel_id=1, source_target_pairs={{1,0},{3,2},{5,4},{7,6},{9,8},{11,10},{13,12},{15,14},{17,16},{19,... | collective-permute-start | bytes 3145736 | tf_op jit(solution)/shard_map/ppermute | solution.py:37
  10.4 118.7 %reduce-scatter.4.cloned.1.call-start = ((), (), s32[]{:S(2)}) async-start(), calls=%async_computation.3 | async-start | bytes 2228224
  11.2 0.8 copy-start.9
  12.8 23.8 %copy-start.13 = (bf16[256,128]{1,0:T(8,128)(2,1)S(1)}, bf16[256,128]{1,0:T(8,128)(2,1)}, u32[]{:S(2)}) copy-start(bf16[256,128]{1,0:T(8,128)(2,1)} %constant.17.clone) | copy-start | bytes 196612
  13.5 24.5 %copy-start.2 = (f32[256,4096]{1,0:T(8,128)}, f32[256,4096]{1,0:T(8,128)S(1)}, u32[]{:S(2)}) copy-start(f32[256,4096]{1,0:T(8,128)S(1)} %convolution_add_fusion.2) | copy-start | bytes 12582916
  13.6 23.7 %copy-start.12 = (bf16[256,128]{1,0:T(8,128)(2,1)S(1)}, bf16[256,128]{1,0:T(8,128)(2,1)}, u32[]{:S(2)}) copy-start(bf16[256,128]{1,0:T(8,128)(2,1)} %constant.16.clone) | copy-start | bytes 196612
  52.4 2.0 copy-start.7
  54.4 2.2 %copy-start.3 = (f32[256,4096]{1,0:T(8,128)S(1)}, f32[256,4096]{1,0:T(8,128)}, u32[]{:S(2)}) copy-start(f32[256,4096]{1,0:T(8,128)} %copy-done.2) | copy-start | bytes 12582916
  54.4 2.9 %copy-start.6 = (f32[128,4096]{1,0:T(8,128)S(1)}, f32[128,4096]{1,0:T(8,128)}, u32[]{:S(2)}) copy-start(f32[128,4096]{1,0:T(8,128)} %get-tuple-element.7) | copy-start | bytes 6291460
  57.3 4.2 %copy-start.5 = (f32[128,4096]{1,0:T(8,128)S(1)}, f32[128,4096]{1,0:T(8,128)}, u32[]{:S(2)}) copy-start(f32[128,4096]{1,0:T(8,128)} %get-tuple-element.6) | copy-start | bytes 6291460
  57.3 4.2 %copy-start.8 = (bf16[128,256]{1,0:T(8,128)(2,1)S(1)}, bf16[128,256]{1,0:T(8,128)(2,1)}, u32[]{:S(2)}) copy-start(bf16[128,256]{1,0:T(8,128)(2,1)} %constant.18.clone) | copy-start | bytes 196612
  61.5 0.8 copy-start.11
  68.2 125.9 %all-reduce.2.cloned.1.call-start = ((), (), s32[]{:S(2)}) async-start(), calls=%async_computation.2 | async-start | bytes 4194304 | tf_op jit(solution)/shard_map/psum | solution.py:58
  68.4 2.5 %copy-start.4 = (f32[128,4096]{1,0:T(8,128)S(1)}, f32[128,4096]{1,0:T(8,128)}, u32[]{:S(2)}) copy-start(f32[128,4096]{1,0:T(8,128)} %get-tuple-element.10) | copy-start | bytes 6291460
  194.0 3.1 %copy-start.1 = (bf16[1,128,4096]{2,1,0:T(8,128)(2,1)S(1)}, bf16[1,128,4096]{2,1,0:T(8,128)(2,1)}, u32[]{:S(2)}) copy-start(bf16[1,128,4096]{2,1,0:T(8,128)(2,1)} %param.18) | copy-start | bytes 3145732
Sparse Core Ops, SparseCore 0:
  10.6 41.7 all-gather.1
  68.3 60.7 reduce-scatter.3
  132.1 61.8 all-reduce.1

commit v2 on v1

--- a/solution.py
+++ b/solution.py
@@ -1,9 +1,12 @@
+import functools
 import math
 
 import jax
 import jax.numpy as jnp
 import numpy as np
 from jax import lax
+from jax.experimental import pallas as pl
+from jax.experimental.pallas import tpu as pltpu
 from jax.sharding import PartitionSpec as P
 
 
@@ -24,7 +27,7 @@
     return lax.dot_general(a, b, (((1,), (0,)), ((), ())), preferred_element_type=jnp.float32)
 
 
-def shards(conv_input, gate_value, out_grad, filter_taps):
+def general(conv_input, gate_value, out_grad, filter_taps):
     inputs = conv_input[0]
     rows = inputs.shape[0]
     taps = filter_taps.shape[0] * lax.axis_size("dp")
@@ -60,6 +63,302 @@
     return (grad.astype(jnp.bfloat16)[None], shard_grad * (1.0 / math.sqrt(tokens_all)))
 
 
+CHUNKS = 8
+MESH = pl.DeviceIdType.MESH
+
+
+def kernel(
+    pairs, ranks, scale,
+    in_hbm, gate_hbm, cot_hbm, taps_hbm, fh, fl, bh, bl,
+    out_hbm, fgrad,
+    x_in, x_gate, x_cot, g_ext, taps_all, spec, p32, own32, cbuf, csrc, rbuf, sbuf, acc, xbuf, obuf,
+    ld_in, ld_gate, ld_cot, ld_taps, st_out,
+    rim_s, rim_r, tap_s, tap_f, tap_r, c_s, c_r, s_s, s_r, x_s, x_r,
+):
+    dp, ctx = lax.axis_index("dp"), lax.axis_index("ctx")
+    core, mine = lax.rem(dp, 2), dp // 2
+    partner = dp + 1 - 2 * core
+    rows, channels = x_in.shape
+    wide = channels // CHUNKS
+    last = ctx == ranks - 1
+
+    def cols(c):
+        return pl.ds(pl.multiple_of(c * wide, wide), wide)
+
+    def load(src, dst, sem, c):
+        return pltpu.make_async_copy(src.at[:, cols(c)], dst.at[:, cols(c)], sem.at[c])
+
+    def each(n, body, start=0):
+        lax.fori_loop(start, n, lambda i, z: (body(i), z)[1], 0)
+
+    own_taps = pltpu.make_async_copy(taps_hbm, taps_all.at[dp], ld_taps)
+
+    def first_loads(c):
+        load(cot_hbm, x_cot, ld_cot, c).start()
+        load(gate_hbm, x_gate, ld_gate, c).start()
+
+    each(CHUNKS, first_loads)
+    own_taps.start()
+    each(CHUNKS, lambda c: load(in_hbm, x_in, ld_in, c).start())
+
+    def peer(k):
+        return lax.rem(mine + k, pairs)
+
+    def rank(k):
+        return lax.rem(ctx + k, ranks)
+
+    barrier = pltpu.get_barrier_semaphore()
+    pl.semaphore_signal(barrier, inc=1, device_id=(partner, ctx), device_id_type=MESH)
+    for k in range(1, pairs):
+        pl.semaphore_signal(barrier, inc=1, device_id=(2 * peer(k) + core, ctx), device_id_type=MESH)
+    for k in range(1, ranks):
+        pl.semaphore_signal(barrier, inc=1, device_id=(dp, rank(k)), device_id_type=MESH)
+    pl.semaphore_wait(barrier, pairs + ranks - 1)
+
+    def remote(src, dst, send, recv, to):
+        return pltpu.make_async_remote_copy(
+            src_ref=src, dst_ref=dst, send_sem=send, recv_sem=recv, device_id=to, device_id_type=MESH
+        )
+
+    def rim(c):
+        return remote(
+            g_ext.at[pl.ds(0, rows), cols(c)], g_ext.at[pl.ds(rows, rows), cols(c)],
+            rim_s.at[c], rim_r.at[c], (dp, lax.max(ctx - 1, 0)),
+        )
+
+    def mix(c):
+        load(cot_hbm, x_cot, ld_cot, c).wait()
+        load(gate_hbm, x_gate, ld_gate, c).wait()
+        a = x_cot[:, cols(c)].astype(jnp.float32)
+        b = x_gate[:, cols(c)].astype(jnp.float32)
+        g_ext[pl.ds(0, rows), cols(c)] = (a * b).astype(jnp.bfloat16)
+
+        @pl.when(ctx > 0)
+        def _():
+            rim(c).start()
+
+        @pl.when(last)
+        def _():
+            g_ext[pl.ds(rows, rows), cols(c)] = jnp.zeros((rows, wide), jnp.bfloat16)
+
+    each(CHUNKS, mix)
+
+    own_taps.wait()
+
+    def tap_send(k):
+        return remote(
+            taps_all.at[dp], taps_all.at[dp], tap_s.at[k], tap_r.at[dp], (2 * peer(k) + core, ctx)
+        )
+
+    def tap_pass(g):
+        shard = taps_all.at[2 * g + core]
+        return remote(shard, shard, tap_f.at[g], tap_r.at[2 * g + core], (partner, ctx))
+
+    def tap_from(g, c):
+        shard = taps_all.at[2 * g + c]
+        return remote(shard, shard, tap_f.at[g], tap_r.at[2 * g + c], (partner, ctx))
+
+    each(pairs, lambda k: tap_send(k).start(), 1)
+    tap_pass(mine).start()
+
+    def pass_taps():
+        def one(k):
+            tap_from(peer(k), core).wait_recv()
+            tap_pass(peer(k)).start()
+
+        each(pairs, one, 1)
+
+    def all_taps():
+        each(pairs, lambda g: tap_from(g, 1 - core).wait_recv())
+
+    def back(value, n):
+        high = value.astype(jnp.bfloat16)
+        low = (value - high.astype(jnp.float32)).astype(jnp.bfloat16)
+        return dot(bh[:n, :], high) + dot(bl[:n, :], high) + dot(bh[:n, :], low)
+
+    half = fh.shape[0] // 2
+
+    def correlate(a, g, n):
+        ar, ai, gr, gi = a[:half], a[half:], g[:half], g[half:]
+        return back(jnp.concatenate([ar * gr + ai * gi, ar * gi - ai * gr], 0), n)
+
+    count = taps_all.shape[1]
+    taps = 2 * pairs * count
+
+    def cross(c):
+        return remote(csrc.at[:, :, cols(c)], cbuf.at[:, :, cols(c)], c_s.at[c], c_r.at[c], (partner, ctx))
+
+    def stage1(c):
+        @pl.when(jnp.logical_not(last))
+        def _():
+            rim(c).wait_recv()
+
+        load(in_hbm, x_in, ld_in, c).wait()
+        ext = g_ext[:, cols(c)]
+        g = dot(fh[...], ext) + dot(fl[...], ext)
+        spec[:, cols(c)] = g
+        u = x_in[:, cols(c)]
+        x = dot(fh[:, :rows], u) + dot(fl[:, :rows], u)
+        p32[...] = correlate(x, g, taps).reshape(pairs, 2, count, wide)
+        csrc[:, :, cols(c)] = p32[:, 1 - core].astype(jnp.bfloat16)
+        own32[:, :, cols(c)] = p32[:, core]
+        cross(c).start()
+
+    def scatter(c, k):
+        return remote(
+            sbuf.at[peer(k), :, cols(c)], rbuf.at[mine, :, cols(c)],
+            s_s.at[k, c], s_r.at[mine, c], (2 * peer(k) + core, ctx),
+        )
+
+    def scattered(c, k):
+        return remote(
+            sbuf.at[peer(k), :, cols(c)], rbuf.at[peer(k), :, cols(c)],
+            s_s.at[k, c], s_r.at[peer(k), c], (2 * peer(k) + core, ctx),
+        )
+
+    def stage2(c):
+        cross(c).wait_recv()
+        total = own32[:, :, cols(c)] + cbuf[:, :, cols(c)].astype(jnp.float32)
+        own32[:, :, cols(c)] = total
+        sbuf[:, :, cols(c)] = total.astype(jnp.bfloat16)
+        for k in range(1, pairs):
+            scatter(c, k).start()
+
+    def swap(c, k):
+        return remote(
+            xbuf.at[ctx, :, cols(c)], xbuf.at[ctx, :, cols(c)], x_s.at[k, c], x_r.at[ctx, c], (dp, rank(k))
+        )
+
+    def swapped(c, k):
+        slot = xbuf.at[rank(k), :, cols(c)]
+        return remote(slot, slot, x_s.at[k, c], x_r.at[rank(k), c], (dp, rank(k)))
+
+    def stage3(c):
+        total = own32[mine, :, cols(c)]
+        for k in range(1, pairs):
+            scattered(c, k).wait_recv()
+            total = total + rbuf[peer(k), :, cols(c)].astype(jnp.float32)
+        xbuf[ctx, :, cols(c)] = total.astype(jnp.bfloat16)
+        for k in range(1, ranks):
+            swap(c, k).start()
+
+    def put(c):
+        return pltpu.make_async_copy(obuf.at[:, cols(c)], out_hbm.at[:, cols(c)], st_out.at[c])
+
+    def grad(c):
+        t = taps_all[:, :, cols(c)].astype(jnp.float32).reshape(taps, wide).astype(jnp.bfloat16)
+        h = dot(fh[:, :taps], t) + dot(fl[:, :taps], t)
+        obuf[:, cols(c)] = correlate(h, spec[:, cols(c)], rows).astype(jnp.bfloat16)
+        put(c).start()
+
+    middle = CHUNKS // 2
+
+    def step(c):
+        stage1(c)
+
+        @pl.when(c >= 1)
+        def _():
+            stage2(c - 1)
+
+        @pl.when(c >= 2)
+        def _():
+            stage3(c - 2)
+
+        @pl.when(c == middle - 1)
+        def _():
+            pass_taps()
+
+        @pl.when(c == middle)
+        def _():
+            all_taps()
+
+        @pl.when(c >= middle)
+        def _():
+            each(2 * (c - middle) + 2, grad, 2 * (c - middle))
+
+    each(CHUNKS, step)
+    stage2(CHUNKS - 1)
+    stage3(CHUNKS - 2)
+    stage3(CHUNKS - 1)
+
+    def finish(c):
+        for k in range(1, ranks):
+            swapped(c, k).wait_recv()
+        total = xbuf[0, :, cols(c)].astype(jnp.float32)
+        for r in range(1, ranks):
+            total = total + xbuf[r, :, cols(c)].astype(jnp.float32)
+        fgrad[:, cols(c)] = total * scale
+
+    each(CHUNKS, finish)
+
+    def drain(c):
+        put(c).wait()
+        cross(c).wait_send()
+        for k in range(1, pairs):
+            scatter(c, k).wait_send()
+        for k in range(1, ranks):
+            swap(c, k).wait_send()
+
+        @pl.when(ctx > 0)
+        def _():
+            rim(c).wait_send()
+
+    each(CHUNKS, drain)
+    each(pairs, lambda k: tap_send(k).wait_send(), 1)
+    each(pairs, lambda g: tap_pass(g).wait_send())
+
+
+def shards(conv_input, gate_value, out_grad, filter_taps):
+    _, rows, channels = conv_input.shape
+    count = filter_taps.shape[0]
+    members, ranks = lax.axis_size("dp"), lax.axis_size("ctx")
+    taps = count * members
+    wide = channels // CHUNKS
+    if count % 8 or taps != rows or rows % 16 or members % 2 or channels % (128 * CHUNKS):
+        return general(conv_input, gate_value, out_grad, filter_taps)
+    pairs = members // 2
+    scale = 1.0 / math.sqrt(rows * ranks * members)
+    (fh, fl), (bh, bl) = transforms(rows + taps)
+    hbm, vmem = pl.BlockSpec(memory_space=pl.ANY), pl.BlockSpec(memory_space=pltpu.VMEM)
+    bf, f32, dma = jnp.bfloat16, jnp.float32, pltpu.SemaphoreType.DMA
+    out, fgrad = pl.pallas_call(
+        functools.partial(kernel, pairs, ranks, scale),
+        out_shape=(
+            jax.ShapeDtypeStruct((rows, channels), bf),
+            jax.ShapeDtypeStruct((count, channels), f32),
+        ),
+        in_specs=[hbm] * 4 + [vmem] * 4,
+        out_specs=(hbm, vmem),
+        scratch_shapes=[
+            pltpu.VMEM((rows, channels), bf),
+            pltpu.VMEM((rows, channels), bf),
+            pltpu.VMEM((rows, channels), bf),
+            pltpu.VMEM((2 * rows, channels), bf),
+            pltpu.VMEM((members, count, channels), bf),
+            pltpu.VMEM((rows + taps, channels), f32),
+            pltpu.VMEM((pairs, 2, count, wide), f32),
+            pltpu.VMEM((pairs, count, channels), f32),
+            pltpu.VMEM((pairs, count, channels), bf),
+            pltpu.VMEM((pairs, count, channels), bf),
+            pltpu.VMEM((pairs, count, channels), bf),
+            pltpu.VMEM((pairs, count, channels), bf),
+            pltpu.VMEM((count, channels), f32),
+            pltpu.VMEM((ranks, count, channels), bf),
+            pltpu.VMEM((rows, channels), bf),
+            dma((CHUNKS,)), dma((CHUNKS,)), dma((CHUNKS,)), dma, dma((CHUNKS,)),
+            dma((CHUNKS,)), dma((CHUNKS,)),
+            dma((pairs,)), dma((pairs,)), dma((members,)),
+            dma((CHUNKS,)), dma((CHUNKS,)),
+            dma((pairs, CHUNKS)), dma((pairs, CHUNKS)),
+            dma((ranks, CHUNKS)), dma((ranks, CHUNKS)),
+        ],
+        compiler_params=pltpu.CompilerParams(
+            collective_id=0, has_side_effects=True, vmem_limit_bytes=40 * 2**20
+        ),
+    )(conv_input[0], gate_value[0], out_grad[0], filter_taps, *map(jnp.asarray, (fh, fl, bh, bl)))
+    return out[None], fgrad
+
+
 def solution(mesh):
     in_specs = (P("dp", "ctx", None), P("dp", "ctx", None), P("dp", "ctx", None), P("dp", None))
     out_specs = (P("dp", "ctx", None), P("dp", None))

time: 204 us -> 58 us (0.28)
  waiting for transfers between devices: 148 us -> 0 us
  Pallas kernels: 0 us -> 47.2 us
  matrix products: 18.2 us -> 0 us
  between operations: 14 us -> 0.65 us
  other arithmetic: 11.1 us -> 0 us
    psum x1 -> x0, waiting for transfers between devices: 57.7 us -> none  [shards(): lax.psum(lax.psum_scatter(partial, 'dp', scatter_dimension=0, tiled=True)...]
    unnamed x4 -> x0, waiting for transfers between devices: 56.1 us -> none
    pallas_call x0 -> x1, Pallas kernels: none -> 47.2 us  [shards(): pl.pallas_call(functools.partial(kernel, pairs, ranks, scale), out_shape=...]
    ppermute x1 -> x0, waiting for transfers between devices: 23 us -> none  [shards(): lax.ppermute(mixed[:taps], 'ctx', [(i + 1, i) for i in range(devices - 1)])]
    dot_general x14 -> x0, matrix products: 18.2 us -> none  [dot(): lax.dot_general(a, b, (((1,), (0,)), ((), ())), preferred_element_type=jn...]
    all_gather x1 -> x0, waiting for transfers between devices: 11.2 us -> none  [shards(): full_taps = lax.all_gather(filter_taps, 'dp', axis=0, tiled=True)]
    add x2 -> x0, other arithmetic: 7.41 us -> none  [the longest x1 4.21 us: shards(): grad = back(hr * gr + hi * gi, hr * gi - hi * gr, rows)]
    unnamed x32 -> x18, local copies, waits for them, and re-layouts: 10.7 us -> 9.75 us
  transfers between devices with their start and end apart: 4 -> 0, of which waited for: 4 -> 0; matrix products, arithmetic and copies ran while one was open for 8% -> 0% of each run, Pallas kernels for 0% -> 0%
where the time goes in v2:
time: 58 us; the launch traced here: 57.6 us
  Pallas kernels  47.2 us (81%)
  local copies, waits for them, and re-layouts  9.75 us (17%)
  between operations  0.65 us (1%)
    pallas_call x1, Pallas kernels, shards(): pl.pallas_call(functools.partial(kernel, pairs, ranks, scale), out_shape=...  47.2 us
    unnamed x18, local copies, waits for them, and re-layouts  9.75 us

profile of v2, /device:TPU:0, one launch (start us, length us, event | category | flops | bytes accessed | tf_op | source)
XLA Modules:
  0.0 57.6 jit_solution(15781993464996099900)
XLA Ops:
  0.6 0.0 copy-start
  0.6 1.2 %copy-done = bf16[1,128,4096]{2,1,0:T(8,128)(2,1)S(1)} copy-done((bf16[1,128,4096]{2,1,0:T(8,128)(2,1)S(1)}, bf16[1,128,4096]{2,1,0:T(8,128)(2,1)}, u32[]{:S(2)}) %copy-start) | copy-done | bytes 1048600
  1.9 0.0 copy-start.1
  1.9 1.2 %copy-done.1 = bf16[1,128,4096]{2,1,0:T(8,128)(2,1)S(1)} copy-done((bf16[1,128,4096]{2,1,0:T(8,128)(2,1)S(1)}, bf16[1,128,4096]{2,1,0:T(8,128)(2,1)}, u32[]{:S(2)}) %copy-start.1) | copy-done | bytes 1048600
  3.1 0.0 copy-start.2
  3.1 1.2 %copy-done.2 = bf16[1,128,4096]{2,1,0:T(8,128)(2,1)S(1)} copy-done((bf16[1,128,4096]{2,1,0:T(8,128)(2,1)S(1)}, bf16[1,128,4096]{2,1,0:T(8,128)(2,1)}, u32[]{:S(2)}) %copy-start.2) | copy-done | bytes 1048600
  4.3 0.0 copy-start.3
  4.3 0.9 %copy-done.3 = bf16[256,256]{1,0:T(8,128)(2,1)S(1)} copy-done((bf16[256,256]{1,0:T(8,128)(2,1)S(1)}, bf16[256,256]{1,0:T(8,128)(2,1)}, u32[]{:S(2)}) %copy-start.3) | copy-done | bytes 131096
  5.2 0.0 copy-start.4
  5.2 0.9 %copy-done.4 = bf16[256,256]{1,0:T(8,128)(2,1)S(1)} copy-done((bf16[256,256]{1,0:T(8,128)(2,1)S(1)}, bf16[256,256]{1,0:T(8,128)(2,1)}, u32[]{:S(2)}) %copy-start.4) | copy-done | bytes 131096
  6.1 0.0 copy-start.5
  6.1 0.9 %copy-done.5 = bf16[256,256]{1,0:T(8,128)(2,1)S(1)} copy-done((bf16[256,256]{1,0:T(8,128)(2,1)S(1)}, bf16[256,256]{1,0:T(8,128)(2,1)}, u32[]{:S(2)}) %copy-start.5) | copy-done | bytes 131096
  7.0 0.0 copy-start.6
  7.0 0.9 %copy-done.6 = bf16[256,256]{1,0:T(8,128)(2,1)S(1)} copy-done((bf16[256,256]{1,0:T(8,128)(2,1)S(1)}, bf16[256,256]{1,0:T(8,128)(2,1)}, u32[]{:S(2)}) %copy-start.6) | copy-done | bytes 131096
  7.9 0.0 copy-start.7
  7.9 0.8 %copy-done.7 = bf16[8,4096]{1,0:T(8,128)(2,1)S(1)} copy-done((bf16[8,4096]{1,0:T(8,128)(2,1)S(1)}, bf16[8,4096]{1,0:T(8,128)(2,1)}, u32[]{:S(2)}) %copy-start.7) | copy-done | bytes 65560
  8.8 47.2 %shard_map.95 = (bf16[128,4096]{1,0:T(8,128)(2,1)S(1)}, f32[8,4096]{1,0:T(8,128)S(1)}) custom-call(bf16[128,4096]{1,0:T(8,128)(2,1)S(1)} %bitcast.4, bf16[128,4096]{1,0:T(8,128)(2,1)S(1)} %bitcast.5, bf16[128,4096]{1,0:T(8,128)(2,1)S(1)} %bitcast.6, bf16[8,4096]{1,0:T(8,128)(2,1)S(1)} %copy-done.7, bf16[256,256]{1,0:T(8,128)(2,1)S(1)} %copy-done.6, ...), custom_call_target="tpu_custom_call" | custom-call | tf_op jit(solution)/shard_map/pallas_call | solution.py:324
  56.0 1.0 %copy.12 = bf16[1,128,4096]{2,1,0:T(8,128)(2,1)} copy(bf16[1,128,4096]{2,1,0:T(8,128)(2,1)S(1)} %bitcast.7) | data formatting | bytes 2097152
  57.0 0.7 %copy.13 = f32[8,4096]{1,0:T(8,128)} copy(f32[8,4096]{1,0:T(8,128)S(1)} %get-tuple-element.9) | data formatting | bytes 262144
Async XLA Ops:
  0.6 1.2 %copy-start = (bf16[1,128,4096]{2,1,0:T(8,128)(2,1)S(1)}, bf16[1,128,4096]{2,1,0:T(8,128)(2,1)}, u32[]{:S(2)}) copy-start(bf16[1,128,4096]{2,1,0:T(8,128)(2,1)} %param.8) | copy-start | bytes 3145732
  1.9 1.2 %copy-start.1 = (bf16[1,128,4096]{2,1,0:T(8,128)(2,1)S(1)}, bf16[1,128,4096]{2,1,0:T(8,128)(2,1)}, u32[]{:S(2)}) copy-start(bf16[1,128,4096]{2,1,0:T(8,128)(2,1)} %param.9) | copy-start | bytes 3145732
  3.1 1.2 %copy-start.2 = (bf16[1,128,4096]{2,1,0:T(8,128)(2,1)S(1)}, bf16[1,128,4096]{2,1,0:T(8,128)(2,1)}, u32[]{:S(2)}) copy-start(bf16[1,128,4096]{2,1,0:T(8,128)(2,1)} %param.10) | copy-start | bytes 3145732
  4.3 0.9 %copy-start.3 = (bf16[256,256]{1,0:T(8,128)(2,1)S(1)}, bf16[256,256]{1,0:T(8,128)(2,1)}, u32[]{:S(2)}) copy-start(bf16[256,256]{1,0:T(8,128)(2,1)} %constant.11.clone.bl) | copy-start | bytes 393220
  5.2 0.9 %copy-start.4 = (bf16[256,256]{1,0:T(8,128)(2,1)S(1)}, bf16[256,256]{1,0:T(8,128)(2,1)}, u32[]{:S(2)}) copy-start(bf16[256,256]{1,0:T(8,128)(2,1)} %constant.10.clone.bh) | copy-start | bytes 393220
  6.1 0.9 %copy-start.5 = (bf16[256,256]{1,0:T(8,128)(2,1)S(1)}, bf16[256,256]{1,0:T(8,128)(2,1)}, u32[]{:S(2)}) copy-start(bf16[256,256]{1,0:T(8,128)(2,1)} %constant.9.clone.fl) | copy-start | bytes 393220
  7.0 0.9 %copy-start.6 = (bf16[256,256]{1,0:T(8,128)(2,1)S(1)}, bf16[256,256]{1,0:T(8,128)(2,1)}, u32[]{:S(2)}) copy-start(bf16[256,256]{1,0:T(8,128)(2,1)} %constant.8.clone.fh) | copy-start | bytes 393220
  7.9 0.8 %copy-start.7 = (bf16[8,4096]{1,0:T(8,128)(2,1)S(1)}, bf16[8,4096]{1,0:T(8,128)(2,1)}, u32[]{:S(2)}) copy-start(bf16[8,4096]{1,0:T(8,128)(2,1)} %taps_hbm.1) | copy-start | bytes 196612

commit v3 on v1

--- a/solution.py
+++ b/solution.py
@@ -1,9 +1,12 @@
+import functools
 import math
 
 import jax
 import jax.numpy as jnp
 import numpy as np
 from jax import lax
+from jax.experimental import pallas as pl
+from jax.experimental.pallas import tpu as pltpu
 from jax.sharding import PartitionSpec as P
 
 
@@ -24,7 +27,7 @@
     return lax.dot_general(a, b, (((1,), (0,)), ((), ())), preferred_element_type=jnp.float32)
 
 
-def shards(conv_input, gate_value, out_grad, filter_taps):
+def general(conv_input, gate_value, out_grad, filter_taps):
     inputs = conv_input[0]
     rows = inputs.shape[0]
     taps = filter_taps.shape[0] * lax.axis_size("dp")
@@ -60,6 +63,389 @@
     return (grad.astype(jnp.bfloat16)[None], shard_grad * (1.0 / math.sqrt(tokens_all)))
 
 
+CHUNKS = 8
+MESH = pl.DeviceIdType.MESH
+
+
+def kernel(
+    pairs, ranks, scale,
+    in_hbm, gate_hbm, cot_hbm, taps_hbm, f_hbm, b_hbm,
+    out_hbm, fgrad_hbm,
+    x_gate, x_cot, x_ext, g_ext, taps_all, f_all, b_all, p32, own32, csrc, cbuf, half32, ysrc, ybuf,
+    zsrc, zbuf, xbuf, obuf, fbuf,
+    ld_in, ld_gate, ld_cot, ld_taps, ld_f, st_out, st_f,
+    rim_s, rim_r, in_s, in_r, tz_s, ty_s, tc_s, tap_r,
+    c_s, c_r, y_s, y_r, z_s, z_r, x_s, x_r,
+):
+    dp, ctx = lax.axis_index("dp"), lax.axis_index("ctx")
+    core, mine = lax.rem(dp, 2), dp // 2
+    partner = dp + 1 - 2 * core
+    side, place, places = lax.rem(mine, 2), mine // 2, pairs // 2
+    across = 2 * (mine + 1 - 2 * side) + core
+    rows, channels = x_gate.shape
+    wide = channels // CHUNKS
+    middle = CHUNKS // 2
+    last, first = ctx == ranks - 1, ctx == 0
+    left, right = lax.max(ctx - 1, 0), lax.min(ctx + 1, ranks - 1)
+    upper, lower = pl.ds(0, rows), pl.ds(rows, rows)
+
+    def cols(c):
+        return pl.ds(pl.multiple_of(c * wide, wide), wide)
+
+    def load(src, dst, sem, c):
+        return pltpu.make_async_copy(src.at[:, cols(c)], dst.at[:, cols(c)], sem.at[c])
+
+    def load_in(c):
+        return pltpu.make_async_copy(in_hbm.at[:, cols(c)], x_ext.at[lower, cols(c)], ld_in.at[c])
+
+    def each(n, body, start=0):
+        lax.fori_loop(start, n, lambda i, z: (body(i), z)[1], 0)
+
+    own_taps = pltpu.make_async_copy(taps_hbm, taps_all.at[dp], ld_taps)
+    load_f = pltpu.make_async_copy(f_hbm, f_all, ld_f.at[0])
+    load_b = pltpu.make_async_copy(b_hbm, b_all, ld_f.at[1])
+
+    def loads(c):
+        load(cot_hbm, x_cot, ld_cot, c).start()
+        load(gate_hbm, x_gate, ld_gate, c).start()
+
+    each(CHUNKS, loads)
+    own_taps.start()
+    load_f.start()
+    load_b.start()
+    each(CHUNKS, lambda c: load_in(c).start())
+
+    def z_peer(k):
+        return lax.rem(place + k, places)
+
+    def z_device(k):
+        return 4 * z_peer(k) + 2 * side + core
+
+    def rank(k):
+        return lax.rem(ctx + k, ranks)
+
+    barrier = pltpu.get_barrier_semaphore()
+    pl.semaphore_signal(barrier, inc=1, device_id=(partner, ctx), device_id_type=MESH)
+    pl.semaphore_signal(barrier, inc=1, device_id=(across, ctx), device_id_type=MESH)
+    for k in range(1, places):
+        pl.semaphore_signal(barrier, inc=1, device_id=(z_device(k), ctx), device_id_type=MESH)
+    for k in range(1, ranks):
+        pl.semaphore_signal(barrier, inc=1, device_id=(dp, rank(k)), device_id_type=MESH)
+    pl.semaphore_wait(barrier, places + ranks)
+
+    def remote(src, dst, send, recv, to):
+        return pltpu.make_async_remote_copy(
+            src_ref=src, dst_ref=dst, send_sem=send, recv_sem=recv, device_id=to, device_id_type=MESH
+        )
+
+    def rim(c):
+        return remote(g_ext.at[upper, cols(c)], g_ext.at[lower, cols(c)], rim_s.at[c], rim_r.at[c], (dp, left))
+
+    def lend(c):
+        return remote(in_hbm.at[:, cols(c)], x_ext.at[upper, cols(c)], in_s.at[c], in_r.at[c], (dp, right))
+
+    def mix(c):
+        load(cot_hbm, x_cot, ld_cot, c).wait()
+        load(gate_hbm, x_gate, ld_gate, c).wait()
+        a = x_cot[:, cols(c)].astype(jnp.float32)
+        b = x_gate[:, cols(c)].astype(jnp.float32)
+        g_ext[upper, cols(c)] = (a * b).astype(jnp.bfloat16)
+
+        @pl.when(ctx > 0)
+        def _():
+            rim(c).start()
+
+    @pl.when(jnp.logical_not(last))
+    def _():
+        each(CHUNKS, lambda c: lend(c).start(), middle)
+
+    each(CHUNKS, mix)
+
+    def shard(p, s, c):
+        return taps_all.at[4 * p + 2 * s + c]
+
+    def tap(p, s, c, sem, to):
+        return remote(shard(p, s, c), shard(p, s, c), sem, tap_r.at[4 * p + 2 * s + c], (to, ctx))
+
+    def tap_z(k):
+        return tap(place, side, core, tz_s.at[k], z_device(k))
+
+    def tap_y(p):
+        return tap(p, side, core, ty_s.at[p], across)
+
+    def tap_c(p, s):
+        return tap(p, s, core, tc_s.at[p, s], partner)
+
+    def tap_wait(p, s, c):
+        tap(p, s, c, ty_s.at[p], partner).wait_recv()
+
+    own_taps.wait()
+    each(places, lambda k: tap_z(k).start(), 1)
+    tap_y(place).start()
+    tap_c(place, side).start()
+
+    def pass_y():
+        def one(k):
+            tap_wait(z_peer(k), side, core)
+            tap_y(z_peer(k)).start()
+            tap_c(z_peer(k), side).start()
+
+        each(places, one, 1)
+
+    def pass_c():
+        def one(p):
+            tap_wait(p, 1 - side, core)
+            tap_c(p, 1 - side).start()
+
+        each(places, one)
+
+    def all_taps():
+        def one(p):
+            tap_wait(p, 0, 1 - core)
+            tap_wait(p, 1, 1 - core)
+
+        each(places, one)
+
+    @pl.when(last)
+    def _():
+        g_ext[lower, :] = jnp.zeros((rows, channels), jnp.bfloat16)
+
+    @pl.when(first)
+    def _():
+        x_ext[upper, :] = jnp.zeros((rows, channels), jnp.bfloat16)
+
+    load_f.wait()
+    load_b.wait()
+
+    def ahead(x):
+        n = x.shape[0]
+        return dot(f_all[0, :, :n], x) + dot(f_all[1, :, :n], x)
+
+    def later(x):
+        return dot(f_all[0, :, rows:], x) + dot(f_all[1, :, rows:], x)
+
+    def back(value, n):
+        high = value.astype(jnp.bfloat16)
+        low = (value - high.astype(jnp.float32)).astype(jnp.bfloat16)
+        return dot(b_all[0, :n, :], high) + dot(b_all[1, :n, :], high) + dot(b_all[0, :n, :], low)
+
+    half = f_all.shape[1] // 2
+
+    def correlate(a, g, n):
+        ar, ai, gr, gi = a[:half], a[half:], g[:half], g[half:]
+        return back(jnp.concatenate([ar * gr + ai * gi, ar * gi - ai * gr], 0), n)
+
+    count = taps_all.shape[1]
+    taps = 2 * pairs * count
+    f32, bf = jnp.float32, jnp.bfloat16
+
+    def chunk(i):
+        return jnp.where(last, i, lax.rem(i + middle, CHUNKS))
+
+    def cross(c):
+        return remote(csrc.at[:, :, cols(c)], cbuf.at[:, :, cols(c)], c_s.at[c], c_r.at[c], (partner, ctx))
+
+    def turn(c):
+        return remote(ysrc.at[:, :, cols(c)], ybuf.at[:, :, cols(c)], y_s.at[c], y_r.at[c], (across, ctx))
+
+    def spread(c, k):
+        return remote(
+            zsrc.at[z_peer(k), :, cols(c)], zbuf.at[place, :, cols(c)],
+            z_s.at[k, c], z_r.at[place, c], (z_device(k), ctx),
+        )
+
+    def gathered(c, k):
+        slot = zbuf.at[z_peer(k), :, cols(c)]
+        return remote(slot, slot, z_s.at[k, c], z_r.at[z_peer(k), c], (z_device(k), ctx))
+
+    def swap(c, k):
+        slot = xbuf.at[ctx, :, cols(c)]
+        return remote(slot, slot, x_s.at[k, c], x_r.at[ctx, c], (dp, rank(k)))
+
+    def swapped(c, k):
+        slot = xbuf.at[rank(k), :, cols(c)]
+        return remote(slot, slot, x_s.at[k, c], x_r.at[rank(k), c], (dp, rank(k)))
+
+    def stage1(c):
+        load_in(c).wait()
+
+        @pl.when(c < middle)
+        def _():
+            @pl.when(jnp.logical_not(last))
+            def _():
+                rim(c).wait_recv()
+
+            p = correlate(ahead(x_ext[lower, cols(c)]), ahead(g_ext[:, cols(c)]), taps)
+            p32[...] = p.reshape(places, 2, 2, count, wide)
+
+        @pl.when(c >= middle)
+        def _():
+            @pl.when(jnp.logical_not(first))
+            def _():
+                lend(c).wait_recv()
+
+            p = correlate(ahead(x_ext[:, cols(c)]), later(g_ext[upper, cols(c)]), taps)
+            p32[...] = p.reshape(places, 2, 2, count, wide)
+
+        for s in range(2):
+            csrc[pl.ds(s * places, places), :, cols(c)] = p32[:, s, 1 - core].astype(bf)
+            own32[pl.ds(s * places, places), :, cols(c)] = p32[:, s, core]
+        cross(c).start()
+
+    def stage2(c):
+        cross(c).wait_recv()
+        there, here = pl.ds((1 - side) * places, places), pl.ds(side * places, places)
+        ysrc[:, :, cols(c)] = (own32[there, :, cols(c)] + cbuf[there, :, cols(c)].astype(f32)).astype(bf)
+        turn(c).start()
+        half32[:, :, cols(c)] = own32[here, :, cols(c)] + cbuf[here, :, cols(c)].astype(f32)
+
+    def stage3(c):
+        turn(c).wait_recv()
+        total = half32[:, :, cols(c)] + ybuf[:, :, cols(c)].astype(f32)
+        half32[:, :, cols(c)] = total
+        zsrc[:, :, cols(c)] = total.astype(bf)
+        for k in range(1, places):
+            spread(c, k).start()
+
+    def stage4(c):
+        total = half32[place, :, cols(c)]
+        for k in range(1, places):
+            gathered(c, k).wait_recv()
+            total = total + zbuf[z_peer(k), :, cols(c)].astype(f32)
+        xbuf[ctx, :, cols(c)] = total.astype(bf)
+        for k in range(1, ranks):
+            swap(c, k).start()
+
+    def finish(c):
+        for k in range(1, ranks):
+            swapped(c, k).wait_recv()
+        total = xbuf[0, :, cols(c)].astype(f32)
+        for r in range(1, ranks):
+            total = total + xbuf[r, :, cols(c)].astype(f32)
+        fbuf[:, cols(c)] = total * scale
+
+    def put(c):
+        return pltpu.make_async_copy(obuf.at[:, cols(c)], out_hbm.at[:, cols(c)], st_out.at[c])
+
+    put_f = pltpu.make_async_copy(fbuf, fgrad_hbm, st_f)
+
+    def grad(c):
+        @pl.when(jnp.logical_and(c >= middle, jnp.logical_not(last)))
+        def _():
+            rim(c).wait_recv()
+
+        t = taps_all[:, :, cols(c)].astype(f32).reshape(taps, wide).astype(bf)
+        obuf[:, cols(c)] = correlate(ahead(t), ahead(g_ext[:, cols(c)]), rows).astype(bf)
+        put(c).start()
+
+    def step(i):
+        for lag, stage in enumerate((stage1, stage2, stage3, stage4)):
+            @pl.when(jnp.logical_and(i >= lag, i < CHUNKS + lag))
+            def _(lag=lag, stage=stage):
+                stage(chunk(i - lag))
+
+        for when, action in ((2, pass_y), (middle + 1, pass_c), (CHUNKS - 1, all_taps)):
+            @pl.when(i == when)
+            def _(action=action):
+                action()
+
+        @pl.when(i >= CHUNKS - 1)
+        def _():
+            grad(i - CHUNKS + 1)
+
+        @pl.when(i == CHUNKS + 5)
+        def _():
+            each(CHUNKS, finish)
+            put_f.start()
+
+    each(2 * CHUNKS - 1, step)
+
+    def drain(c):
+        put(c).wait()
+        cross(c).wait_send()
+        turn(c).wait_send()
+        for k in range(1, places):
+            spread(c, k).wait_send()
+        for k in range(1, ranks):
+            swap(c, k).wait_send()
+
+        @pl.when(ctx > 0)
+        def _():
+            rim(c).wait_send()
+
+    each(CHUNKS, drain)
+
+    @pl.when(jnp.logical_not(last))
+    def _():
+        each(CHUNKS, lambda c: lend(c).wait_send(), middle)
+
+    each(places, lambda k: tap_z(k).wait_send(), 1)
+
+    def drain_taps(p):
+        tap_y(p).wait_send()
+        tap_c(p, 0).wait_send()
+        tap_c(p, 1).wait_send()
+
+    each(places, drain_taps)
+    put_f.wait()
+
+
+def shards(conv_input, gate_value, out_grad, filter_taps):
+    _, rows, channels = conv_input.shape
+    count = filter_taps.shape[0]
+    members, ranks = lax.axis_size("dp"), lax.axis_size("ctx")
+    taps = count * members
+    wide = channels // CHUNKS
+    if count % 8 or taps != rows or rows % 16 or members % 4 or channels % (128 * CHUNKS):
+        return general(conv_input, gate_value, out_grad, filter_taps)
+    pairs = members // 2
+    places = pairs // 2
+    scale = 1.0 / math.sqrt(rows * ranks * members)
+    forward, inverse = transforms(rows + taps)
+    hbm = pl.BlockSpec(memory_space=pl.ANY)
+    bf, f32, dma, vmem = jnp.bfloat16, jnp.float32, pltpu.SemaphoreType.DMA, pltpu.VMEM
+    out, fgrad = pl.pallas_call(
+        functools.partial(kernel, pairs, ranks, scale),
+        out_shape=(
+            jax.ShapeDtypeStruct((rows, channels), bf),
+            jax.ShapeDtypeStruct((count, channels), f32),
+        ),
+        in_specs=[hbm] * 6,
+        out_specs=(hbm, hbm),
+        scratch_shapes=[
+            vmem((rows, channels), bf),
+            vmem((rows, channels), bf),
+            vmem((2 * rows, channels), bf),
+            vmem((2 * rows, channels), bf),
+            vmem((members, count, channels), bf),
+            vmem((2, rows + taps, rows + taps), bf),
+            vmem((2, rows + taps, rows + taps), bf),
+            vmem((places, 2, 2, count, wide), f32),
+            vmem((pairs, count, channels), f32),
+            vmem((pairs, count, channels), bf),
+            vmem((pairs, count, channels), bf),
+            vmem((places, count, channels), f32),
+            vmem((places, count, channels), bf),
+            vmem((places, count, channels), bf),
+            vmem((places, count, channels), bf),
+            vmem((places, count, channels), bf),
+            vmem((ranks, count, channels), bf),
+            vmem((rows, channels), bf),
+            vmem((count, channels), f32),
+            dma((CHUNKS,)), dma((CHUNKS,)), dma((CHUNKS,)), dma, dma((2,)), dma((CHUNKS,)), dma,
+            dma((CHUNKS,)), dma((CHUNKS,)), dma((CHUNKS,)), dma((CHUNKS,)),
+            dma((places,)), dma((places,)), dma((places, 2)), dma((members,)),
+            dma((CHUNKS,)), dma((CHUNKS,)), dma((CHUNKS,)), dma((CHUNKS,)),
+            dma((places, CHUNKS)), dma((places, CHUNKS)),
+            dma((ranks, CHUNKS)), dma((ranks, CHUNKS)),
+        ],
+        compiler_params=pltpu.CompilerParams(
+            collective_id=0, has_side_effects=True, vmem_limit_bytes=67_000_000
+        ),
+    )(conv_input[0], gate_value[0], out_grad[0], filter_taps, jnp.asarray(np.stack(forward)), jnp.asarray(np.stack(inverse)))
+    return out[None], fgrad
+
+
 def solution(mesh):
     in_specs = (P("dp", "ctx", None), P("dp", "ctx", None), P("dp", "ctx", None), P("dp", None))
     out_specs = (P("dp", "ctx", None), P("dp", None))

time: 204 us -> 43.9 us (0.22)
  waiting for transfers between devices: 148 us -> 0 us
  Pallas kernels: 0 us -> 40.1 us
  matrix products: 18.2 us -> 0 us
  between operations: 14 us -> 0.65 us
  other arithmetic: 11.1 us -> 0 us
  local copies, waits for them, and re-layouts: 10.7 us -> 2.98 us
    psum x1 -> x0, waiting for transfers between devices: 57.7 us -> none  [shards(): lax.psum(lax.psum_scatter(partial, 'dp', scatter_dimension=0, tiled=True)...]
    unnamed x4 -> x0, waiting for transfers between devices: 56.1 us -> none
    pallas_call x0 -> x1, Pallas kernels: none -> 40.1 us  [shards(): pl.pallas_call(functools.partial(kernel, pairs, ranks, scale), out_shape=...]
    ppermute x1 -> x0, waiting for transfers between devices: 23 us -> none  [shards(): lax.ppermute(mixed[:taps], 'ctx', [(i + 1, i) for i in range(devices - 1)])]
    dot_general x14 -> x0, matrix products: 18.2 us -> none  [dot(): lax.dot_general(a, b, (((1,), (0,)), ((), ())), preferred_element_type=jn...]
    all_gather x1 -> x0, waiting for transfers between devices: 11.2 us -> none  [shards(): full_taps = lax.all_gather(filter_taps, 'dp', axis=0, tiled=True)]
    unnamed x32 -> x4, local copies, waits for them, and re-layouts: 10.7 us -> 2.98 us
    add x2 -> x0, other arithmetic: 7.41 us -> none  [the longest x1 4.21 us: shards(): grad = back(hr * gr + hi * gi, hr * gi - hi * gr, rows)]
  transfers between devices with their start and end apart: 4 -> 0, of which waited for: 4 -> 0; matrix products, arithmetic and copies ran while one was open for 8% -> 0% of each run, Pallas kernels for 0% -> 0%
where the time goes in v3:
time: 43.9 us; the launch traced here: 43.7 us
  Pallas kernels  40.1 us (91%)
  local copies, waits for them, and re-layouts  2.98 us (7%)
  between operations  0.65 us (1%)
    pallas_call x1, Pallas kernels, shards(): pl.pallas_call(functools.partial(kernel, pairs, ranks, scale), out_shape=...  40.1 us
    unnamed x4, local copies, waits for them, and re-layouts  2.98 us

profile of v3, /device:TPU:0, one launch (start us, length us, event | category | flops | bytes accessed | tf_op | source)
XLA Modules:
  0.0 43.7 jit_solution(8838840373553353375)
XLA Ops:
  0.6 40.1 %shard_map.77 = (bf16[128,4096]{1,0:T(8,128)(2,1)}, f32[8,4096]{1,0:T(8,128)}) custom-call(bf16[128,4096]{1,0:T(8,128)(2,1)} %bitcast.4, bf16[128,4096]{1,0:T(8,128)(2,1)} %bitcast.5, bf16[128,4096]{1,0:T(8,128)(2,1)} %bitcast.6, bf16[8,4096]{1,0:T(8,128)(2,1)} %taps_hbm.1, bf16[2,256,256]{2,1,0:T(8,128)(2,1)} %constant.4.clone.f_hbm, ...), custom_call_target="tpu_custom_call" | custom-call | tf_op jit(solution)/shard_map/pallas_call | solution.py:407
  40.8 0.0 copy-start
  40.8 2.3 %copy.10 = bf16[1,128,4096]{2,1,0:T(8,128)(2,1)} copy(bf16[1,128,4096]{2,1,0:T(8,128)(2,1)} %bitcast.7) | data formatting | bytes 2097152
  43.1 0.0 copy-done
  43.1 0.7 %copy.11 = f32[8,4096]{1,0:T(8,128)} copy(f32[8,4096]{1,0:T(8,128)S(1)} %copy-done) | data formatting | bytes 262144
Async XLA Ops:
  40.8 2.3 %copy-start = (f32[8,4096]{1,0:T(8,128)S(1)}, f32[8,4096]{1,0:T(8,128)}, u32[]{:S(2)}) copy-start(f32[8,4096]{1,0:T(8,128)} %get-tuple-element.9) | copy-start | bytes 393220

commit v4 on v3

--- a/solution.py
+++ b/solution.py
@@ -70,10 +70,10 @@
 def kernel(
     pairs, ranks, scale,
     in_hbm, gate_hbm, cot_hbm, taps_hbm, f_hbm, b_hbm,
-    out_hbm, fgrad_hbm,
+    obuf, fbuf,
     x_gate, x_cot, x_ext, g_ext, taps_all, f_all, b_all, p32, own32, csrc, cbuf, half32, ysrc, ybuf,
-    zsrc, zbuf, xbuf, obuf, fbuf,
-    ld_in, ld_gate, ld_cot, ld_taps, ld_f, st_out, st_f,
+    zsrc, zbuf, xbuf,
+    ld_in, ld_gate, ld_cot, ld_taps, ld_f,
     rim_s, rim_r, in_s, in_r, tz_s, ty_s, tc_s, tap_r,
     c_s, c_r, y_s, y_r, z_s, z_r, x_s, x_r,
 ):
@@ -131,8 +131,6 @@
         pl.semaphore_signal(barrier, inc=1, device_id=(z_device(k), ctx), device_id_type=MESH)
     for k in range(1, ranks):
         pl.semaphore_signal(barrier, inc=1, device_id=(dp, rank(k)), device_id_type=MESH)
-    pl.semaphore_wait(barrier, places + ranks)
-
     def remote(src, dst, send, recv, to):
         return pltpu.make_async_remote_copy(
             src_ref=src, dst_ref=dst, send_sem=send, recv_sem=recv, device_id=to, device_id_type=MESH
@@ -151,15 +149,21 @@
         b = x_gate[:, cols(c)].astype(jnp.float32)
         g_ext[upper, cols(c)] = (a * b).astype(jnp.bfloat16)
 
+    each(middle, mix)
+    pl.semaphore_wait(barrier, places + ranks)
+
+    def send_rim(c):
         @pl.when(ctx > 0)
         def _():
             rim(c).start()
+
+    each(middle, send_rim)
 
     @pl.when(jnp.logical_not(last))
     def _():
         each(CHUNKS, lambda c: lend(c).start(), middle)
 
-    each(CHUNKS, mix)
+    each(CHUNKS, lambda c: (mix(c), send_rim(c)), middle)
 
     def shard(p, s, c):
         return taps_all.at[4 * p + 2 * s + c]
@@ -324,11 +328,6 @@
             total = total + xbuf[r, :, cols(c)].astype(f32)
         fbuf[:, cols(c)] = total * scale
 
-    def put(c):
-        return pltpu.make_async_copy(obuf.at[:, cols(c)], out_hbm.at[:, cols(c)], st_out.at[c])
-
-    put_f = pltpu.make_async_copy(fbuf, fgrad_hbm, st_f)
-
     def grad(c):
         @pl.when(jnp.logical_and(c >= middle, jnp.logical_not(last)))
         def _():
@@ -336,10 +335,9 @@
 
         t = taps_all[:, :, cols(c)].astype(f32).reshape(taps, wide).astype(bf)
         obuf[:, cols(c)] = correlate(ahead(t), ahead(g_ext[:, cols(c)]), rows).astype(bf)
-        put(c).start()
 
     def step(i):
-        for lag, stage in enumerate((stage1, stage2, stage3, stage4)):
+        for lag, stage in list(zip((0, 1, 3, 5), (stage1, stage2, stage3, stage4))):
             @pl.when(jnp.logical_and(i >= lag, i < CHUNKS + lag))
             def _(lag=lag, stage=stage):
                 stage(chunk(i - lag))
@@ -353,15 +351,13 @@
         def _():
             grad(i - CHUNKS + 1)
 
-        @pl.when(i == CHUNKS + 5)
+        @pl.when(i == 2 * CHUNKS - 2)
         def _():
             each(CHUNKS, finish)
-            put_f.start()
 
     each(2 * CHUNKS - 1, step)
 
     def drain(c):
-        put(c).wait()
         cross(c).wait_send()
         turn(c).wait_send()
         for k in range(1, places):
@@ -387,7 +383,6 @@
         tap_c(p, 1).wait_send()
 
     each(places, drain_taps)
-    put_f.wait()
 
 
 def shards(conv_input, gate_value, out_grad, filter_taps):
@@ -411,7 +406,7 @@
             jax.ShapeDtypeStruct((count, channels), f32),
         ),
         in_specs=[hbm] * 6,
-        out_specs=(hbm, hbm),
+        out_specs=(pl.BlockSpec(memory_space=vmem),) * 2,
         scratch_shapes=[
             vmem((rows, channels), bf),
             vmem((rows, channels), bf),
@@ -430,9 +425,7 @@
             vmem((places, count, channels), bf),
             vmem((places, count, channels), bf),
             vmem((ranks, count, channels), bf),
-            vmem((rows, channels), bf),
-            vmem((count, channels), f32),
-            dma((CHUNKS,)), dma((CHUNKS,)), dma((CHUNKS,)), dma, dma((2,)), dma((CHUNKS,)), dma,
+            dma((CHUNKS,)), dma((CHUNKS,)), dma((CHUNKS,)), dma, dma((2,)),
             dma((CHUNKS,)), dma((CHUNKS,)), dma((CHUNKS,)), dma((CHUNKS,)),
             dma((places,)), dma((places,)), dma((places, 2)), dma((members,)),
             dma((CHUNKS,)), dma((CHUNKS,)), dma((CHUNKS,)), dma((CHUNKS,)),
@@ -440,7 +433,7 @@
             dma((ranks, CHUNKS)), dma((ranks, CHUNKS)),
         ],
         compiler_params=pltpu.CompilerParams(
-            collective_id=0, has_side_effects=True, vmem_limit_bytes=67_000_000
+            collective_id=0, has_side_effects=True, vmem_limit_bytes=65_900_000
         ),
     )(conv_input[0], gate_value[0], out_grad[0], filter_taps, jnp.asarray(np.stack(forward)), jnp.asarray(np.stack(inverse)))
     return out[None], fgrad

time: 43.9 us -> 38.3 us (0.87)
  Pallas kernels: 40.1 us -> 34.6 us
    pallas_call x1, Pallas kernels: 40.1 us -> 34.6 us  [shards(): pl.pallas_call(functools.partial(kernel, pairs, ranks, scale), out_shape=...]
where the time goes in v4:
time: 38.3 us; the launch traced here: 38.2 us
  Pallas kernels  34.6 us (90%)
  local copies, waits for them, and re-layouts  2.98 us (8%)
  between operations  0.65 us (2%)
    pallas_call x1, Pallas kernels, shards(): pl.pallas_call(functools.partial(kernel, pairs, ranks, scale), out_shape=...  34.6 us
    unnamed x4, local copies, waits for them, and re-layouts  2.98 us

profile of v4, /device:TPU:0, one launch (start us, length us, event | category | flops | bytes accessed | tf_op | source)
XLA Modules:
  0.0 38.2 jit_solution(11270253703177606620)
XLA Ops:
  0.6 34.6 %shard_map.77 = (bf16[128,4096]{1,0:T(8,128)(2,1)}, f32[8,4096]{1,0:T(8,128)}) custom-call(bf16[128,4096]{1,0:T(8,128)(2,1)} %bitcast.4, bf16[128,4096]{1,0:T(8,128)(2,1)} %bitcast.5, bf16[128,4096]{1,0:T(8,128)(2,1)} %bitcast.6, bf16[8,4096]{1,0:T(8,128)(2,1)} %taps_hbm.1, bf16[2,256,256]{2,1,0:T(8,128)(2,1)} %constant.4.clone.f_hbm, ...), custom_call_target="tpu_custom_call" | custom-call | tf_op jit(solution)/shard_map/pallas_call | solution.py:402
  35.2 0.0 copy-start
  35.2 2.3 %copy.10 = bf16[1,128,4096]{2,1,0:T(8,128)(2,1)} copy(bf16[1,128,4096]{2,1,0:T(8,128)(2,1)} %bitcast.7) | data formatting | bytes 2097152
  37.5 0.0 copy-done
  37.5 0.7 %copy.11 = f32[8,4096]{1,0:T(8,128)} copy(f32[8,4096]{1,0:T(8,128)S(1)} %copy-done) | data formatting | bytes 262144
Async XLA Ops:
  35.2 2.3 %copy-start = (f32[8,4096]{1,0:T(8,128)S(1)}, f32[8,4096]{1,0:T(8,128)}, u32[]{:S(2)}) copy-start(f32[8,4096]{1,0:T(8,128)} %get-tuple-element.9) | copy-start | bytes 393220
